TPU v7x, 512 devices: a whole 4x8x8 slice. The times are simulated.
512 devices in a mesh: req: 128 (over z, x_hi, y), tensor: 4 (over x_lo, core).
Axes of the slice: x: 4 (x_hi: 2, x_lo: 2; x = x_hi * 2 + x_lo), y: 8, z: 8, core: 2. Of those that a mesh axis runs over, the one named last changes fastest.
Arguments:
- tokens: bfloat16 [32768, 2048], P('req'), may hold values from -6 to 6
- segment_ids: int32 [128, 256], P('req'), may hold values from 0 to 7, never falling along the last dimension, each value on 1 to 128 neighbouring positions
- padding: int32 [32768], P('req'), may hold values 0 or 1
- attn_experts: int32 [32768, 2], P('req'), may hold values from 0 to 3, all different within a row
- gain: float32 [2048], replicated, may hold values from 0.1 to 1.9
- w_router: float32 [2048, 4], replicated, may hold values from -0.125 to 0.125
- w_query: bfloat16 [2048, 4096], P('req', 'tensor'), may hold values from -1 to 1
- w_kv: bfloat16 [2048, 2048], P('req', 'tensor'), may hold values from -1 to 1
- w_out: bfloat16 [4096, 2048], P('tensor', 'req'), may hold values from -0.1875 to 0.1875
- page_shift: int32 [16], replicated, may hold values from 0 to 15, as said below
Outputs:
- attended: bfloat16 [32768, 2048], P('req', 'tensor')
- kv_cache: bfloat16 [2048, 16, 2048], P('req', None, 'tensor')
Inputs may be any that keep to these rules, and one draw needn't show every extreme that they name: `segment_ids`: segment ids never fall along a batch; each of the 8 prompts holds at least one token and at most 128. `attn_experts`: the two experts of a token differ. Block j of every batch goes to the owner page_shift[j] places further along req, cyclically, into that owner's block j.
All inputs are finite; a program needn't handle non-finite values. No bound on the sum of `padding` on one device may be relied on, other than what follows from the above.
Results may differ from a plain program's by a relative error of at most 0.013.
Values may be sent and summed in bfloat16 or wider, within the bound.
A program may use at most 64 MiB of HBM per device.

v0:
```python
import jax
import jax.numpy as jnp
from jax import lax
from jax.sharding import PartitionSpec as P

HD = 128
EXPERTS = 4
BITS = 4


def from_behind(value, axis, steps):
    count = lax.axis_size(axis)
    pairs = [(source, (source + steps) % count) for source in range(count)]
    return lax.ppermute(value, axis, pairs)


def rotate(values, position):
    half_size = values.shape[-1] // 2
    freqs = 10000.0 ** (-jnp.arange(half_size, dtype=jnp.float32) / half_size)
    angles = position.astype(jnp.float32)[:, None] * freqs[None, :]
    angles = angles.reshape((values.shape[0],) + (1,) * (values.ndim - 2) + (half_size,))
    cosine = jnp.cos(angles)
    sine = jnp.sin(angles)
    first = values[..., :half_size]
    second = values[..., half_size:]
    return jnp.concatenate(
        [first * cosine - second * sine, second * cosine + first * sine], axis=-1
    )


def allowed_mask(seg_row, pad_row, query_index, key_index):
    allowed = (seg_row[query_index][:, None] == seg_row[key_index][None, :]) & (
        key_index[None, :] <= query_index[:, None]
    )
    return allowed & (
        (pad_row[key_index][None, :] == 1) | (key_index[None, :] == query_index[:, None])
    )


def attend_dense(queries, keys, values, seg_row, pad_row):
    count = queries.shape[0]
    index = jnp.arange(count, dtype=jnp.int32)
    allowed = allowed_mask(seg_row, pad_row, index, index)
    scores = jnp.einsum(
        "tshd,uhd->shtu", queries, keys, preferred_element_type=jnp.float32
    ) / jnp.sqrt(jnp.float32(queries.shape[-1]))
    masked = jnp.where(allowed[None, None], scores, -1e30)
    peak = jnp.max(masked, axis=3, keepdims=True)
    weights = jnp.where(allowed[None, None], jnp.exp(masked - peak), 0.0)
    total = jnp.sum(weights, axis=3)
    summed = jnp.einsum(
        "shtu,uhd->tshd", weights.astype(jnp.bfloat16), values, preferred_element_type=jnp.float32
    )
    return summed / jnp.transpose(total, (2, 0, 1))[:, :, :, None]


def on_device(
    tokens, segment_ids, padding, attn_experts, gain, w_router, w_query, w_kv, w_out, page_shift
):
    count = tokens.shape[0]
    seg_row = segment_ids[0]
    starts = jnp.sum((seg_row[None, :] < seg_row[:, None]).astype(jnp.int32), axis=1)
    position = jnp.arange(count, dtype=jnp.int32) - starts
    x_float = tokens.astype(jnp.float32)
    normed = (
        x_float
        * lax.rsqrt(jnp.mean(x_float * x_float, axis=1, keepdims=True) + 1e-06)
        * gain[None, :]
    ).astype(jnp.bfloat16)
    pad_float = padding.astype(jnp.float32)
    local_heads = w_kv.shape[1] // (2 * HD)

    def add_rows(piece):
        return jnp.dot(normed, piece, preferred_element_type=jnp.float32)

    keyval = add_rows(lax.all_gather(w_kv, "req", axis=0, tiled=True))
    query_all = add_rows(lax.all_gather(w_query, "req", axis=0, tiled=True))
    keyval = keyval.reshape(count, local_heads, 2, HD)
    keys_rot = rotate(keyval[:, :, 0, :], position)
    keyval = (
        jnp.stack([keys_rot, keyval[:, :, 1, :]], axis=2) * pad_float[:, None, None, None]
    ).astype(jnp.bfloat16)
    logits = jnp.dot(normed.astype(jnp.float32), w_router, preferred_element_type=jnp.float32)
    selector = (
        attn_experts[:, :, None] == jnp.arange(EXPERTS, dtype=jnp.int32)[None, None, :]
    ).astype(jnp.float32)
    gates = jnp.einsum("tse,te->ts", selector, jax.nn.sigmoid(logits))
    query_all = rotate(query_all.reshape(count, local_heads, EXPERTS, HD), position)
    queries = jnp.einsum("thed,tse->tshd", query_all, selector).astype(jnp.bfloat16)
    keys_b = keyval[:, :, 0, :]
    values_b = keyval[:, :, 1, :]
    heads_out = attend_dense(queries, keys_b, values_b, seg_row, padding)
    mixed = (
        jnp.einsum("tshd,tse->thed", heads_out * gates[:, :, None, None], selector)
        * pad_float[:, None, None, None]
    )
    mixed = mixed.reshape(count, local_heads * EXPERTS * HD).astype(jnp.bfloat16)
    partial_out = jnp.dot(
        mixed, lax.all_gather(w_out, "req", axis=1, tiled=True), preferred_element_type=jnp.float32
    )
    attended = lax.psum_scatter(
        partial_out.astype(jnp.bfloat16), "tensor", scatter_dimension=1, tiled=True
    )
    page_count = page_shift.shape[0]
    page_size = count // page_count
    pages = keyval.reshape(page_count, page_size, local_heads * 2 * HD)
    for level in range(BITS):
        moved = from_behind(pages, "req", 2**level)
        taken = page_shift // 2**level % 2 == 1
        pages = jnp.where(taken[:, None, None], moved, pages)
    return (attended, pages)


def solution(mesh):
    placed = (
        P("req", None),
        P("req", None),
        P("req"),
        P("req", None),
        P(),
        P(),
        P("req", "tensor"),
        P("req", "tensor"),
        P("tensor", "req"),
        P(),
    )
    return jax.shard_map(
        on_device,
        mesh=mesh,
        in_specs=placed,
        out_specs=(P("req", "tensor"), P("req", None, "tensor")),
        check_vma=False,
    )
```

profile of v0, /device:TPU:1, one launch (start us, length us, event | category | flops | bytes accessed | tf_op | source)
XLA Modules:
  0.0 490.3 jit_solution(6888651575733452197)
XLA Ops:
  7.2 0.7 all-gather.4.cloned.1.call-update
  8.0 0.7 all-gather.6.cloned.1.call-update
  8.7 0.7 all-gather.8.cloned.1.call-update
  9.5 0.7 convert_element_type.50
  10.2 0.8 copy.27
  11.1 2.0 gather_fusion.1
  13.1 2.0 gather_fusion
  15.4 0.5 fusion.15
  16.0 0.9 fusion.22
  17.3 0.5 multiply_cosine_fusion
  17.9 124.8 %all-gather.4.cloned.1.call-done = bf16[2048,512]{1,0:T(8,128)(2,1)} async-done(((bf16[16,512]{1,0:T(8,128)(2,1)}), bf16[2048,512]{1,0:T(8,128)(2,1)}) %all-gather.4.cloned.1.call-update) | async-done | bytes 2097168 | tf_op jit(solution)/shard_map/all_gather | solution.py:76
  142.7 2.3 fusion.46
  146.7 0.4 stack.10
  147.1 134.4 %all-gather.6.cloned.1.call-done = bf16[2048,1024]{1,0:T(8,128)(2,1)} async-done(((bf16[16,1024]{1,0:T(8,128)(2,1)}), bf16[2048,1024]{1,0:T(8,128)(2,1)}) %all-gather.6.cloned.1.call-update) | async-done | bytes 4194320 | tf_op jit(solution)/shard_map/all_gather | solution.py:77
  281.5 3.5 fusion.44
  285.0 0.5 reshape.220
  285.5 0.8 multiply_subtract_fusion
  286.3 1.2 convolution_convert_fusion.1
  287.5 0.6 fusion.49
  288.4 0.4 fusion.12
  289.0 1.4 fusion.10
  290.8 128.7 %all-gather.8.cloned.1.call-done = bf16[1024,2048]{0,1:T(8,128)(2,1)} async-done(((bf16[1024,16]{0,1:T(8,128)(2,1)}), bf16[1024,2048]{0,1:T(8,128)(2,1)}) %all-gather.8.cloned.1.call-update) | async-done | bytes 4194320 | tf_op jit(solution)/shard_map/all_gather | solution.py:99
  419.5 4.4 convolution_convert_fusion
  424.1 2.9 collective-permute-start
  427.0 9.9 %collective-permute-done = bf16[16,16,512]{2,1,0:T(8,128)(2,1)S(1)} collective-permute-done((bf16[16,16,512]{2,1,0:T(8,128)(2,1)S(1)}, bf16[16,16,512]{2,1,0:T(8,128)(2,1)S(1)}, u32[]{:S(2)}, u32[]{:S(2)}) %collective-permute-start) | collective-permute-done | bytes 262176 | tf_op jit(solution)/shard_map/ppermute | solution.py:14
  437.1 1.9 collective-permute-start.1
  439.0 13.9 %collective-permute-done.1 = bf16[16,16,512]{2,1,0:T(8,128)(2,1)S(1)} collective-permute-done((bf16[16,16,512]{2,1,0:T(8,128)(2,1)S(1)}, bf16[16,16,512]{2,1,0:T(8,128)(2,1)S(1)}, u32[]{:S(2)}, u32[]{:S(2)}) %collective-permute-start.1) | collective-permute-done | bytes 262176 | tf_op jit(solution)/shard_map/ppermute | solution.py:14
  453.1 1.9 collective-permute-start.2
  455.0 17.2 %collective-permute-done.2 = bf16[16,16,512]{2,1,0:T(8,128)(2,1)S(1)} collective-permute-done((bf16[16,16,512]{2,1,0:T(8,128)(2,1)S(1)}, bf16[16,16,512]{2,1,0:T(8,128)(2,1)S(1)}, u32[]{:S(2)}, u32[]{:S(2)}) %collective-permute-start.2) | collective-permute-done | bytes 262176 | tf_op jit(solution)/shard_map/ppermute | solution.py:14
  472.3 1.9 collective-permute-start.3
  474.2 8.8 %collective-permute-done.3 = bf16[16,16,512]{2,1,0:T(8,128)(2,1)S(1)} collective-permute-done((bf16[16,16,512]{2,1,0:T(8,128)(2,1)S(1)}, bf16[16,16,512]{2,1,0:T(8,128)(2,1)S(1)}, u32[]{:S(2)}, u32[]{:S(2)}) %collective-permute-start.3) | collective-permute-done | bytes 262176 | tf_op jit(solution)/shard_map/ppermute | solution.py:14
  483.0 0.8 broadcast_select_fusion.3
  (44 shorter events, 4.0 us)
Async XLA Ops:
  7.2 8.2 %copy-start = (f32[2048,4]{0,1:T(4,128)S(1)}, f32[2048,4]{0,1:T(4,128)}, u32[]{:S(2)}) copy-start(f32[2048,4]{0,1:T(4,128)} %param.15) | copy-start | bytes 98308
  7.2 7.9 %copy-start.2 = (bf16[256,2048]{1,0:T(8,128)(2,1)S(1)}, bf16[256,2048]{1,0:T(8,128)(2,1)}, u32[]{:S(2)}) copy-start(bf16[256,2048]{1,0:T(8,128)(2,1)} %param.10) | copy-start | bytes 3145732
  7.2 8.2 %copy-start.4 = (f32[2048]{0:T(1024)S(1)}, f32[2048]{0:T(1024)}, u32[]{:S(2)}) copy-start(f32[2048]{0:T(1024)} %param.14) | copy-start | bytes 24580
  7.2 135.5 %all-gather.4.cloned.1.call-start = ((), (), s32[]{:S(2)}) async-start(), calls=%async_computation.1 | async-start | bytes 2113536 | tf_op jit(solution)/shard_map/all_gather | solution.py:76
  7.9 273.6 %all-gather.6.cloned.1.call-start = ((), (), s32[]{:S(2)}) async-start(), calls=%async_computation.2 | async-start | bytes 4227072 | tf_op jit(solution)/shard_map/all_gather | solution.py:77
  8.7 410.8 %all-gather.8.cloned.1.call-start = ((), (), s32[]{:S(2)}) async-start(), calls=%async_computation.3 | async-start | bytes 4227072 | tf_op jit(solution)/shard_map/all_gather | solution.py:99
  9.4 474.4 %reduce-scatter.2.cloned.1.call-start = ((), (), s32[]{:S(2)}) async-start(), calls=%async_computation.4 | async-start | bytes 1310720 | tf_op jit(solution)/shard_map/reduce_scatter | solution.py:101
  15.0 1.9 copy-start.1
  290.8 136.2 %copy-start.3 = (s32[16]{0:T(128)S(1)}, s32[16]{0:T(128)}, u32[]{:S(2)}) copy-start(s32[16]{0:T(128)} %param.19) | copy-start | bytes 196
  424.1 12.8 %collective-permute-start = (bf16[16,16,512]{2,1,0:T(8,128)(2,1)S(1)}, bf16[16,16,512]{2,1,0:T(8,128)(2,1)S(1)}, u32[]{:S(2)}, u32[]{:S(2)}) collective-permute-start(bf16[16,16,512]{2,1,0:T(8,128)(2,1)S(1)} %multiply_convert_fusion), channel_id=1, source_target_pairs={{0,4},{4,8},{8,12},{12,16},{16,20},{20,24},{24,28},{28,32},{32,36}... | collective-permute-start | bytes 786440 | tf_op jit(solution)/shard_map/ppermute | solution.py:14
  437.1 15.9 %collective-permute-start.1 = (bf16[16,16,512]{2,1,0:T(8,128)(2,1)S(1)}, bf16[16,16,512]{2,1,0:T(8,128)(2,1)S(1)}, u32[]{:S(2)}, u32[]{:S(2)}) collective-permute-start(bf16[16,16,512]{2,1,0:T(8,128)(2,1)S(1)} %broadcast_select_fusion), channel_id=1, source_target_pairs={{0,8},{4,12},{8,16},{12,20},{16,24},{20,28},{24,32},{28,36},{32,40... | collective-permute-start | bytes 786440 | tf_op jit(solution)/shard_map/ppermute | solution.py:14
  453.1 19.1 %collective-permute-start.2 = (bf16[16,16,512]{2,1,0:T(8,128)(2,1)S(1)}, bf16[16,16,512]{2,1,0:T(8,128)(2,1)S(1)}, u32[]{:S(2)}, u32[]{:S(2)}) collective-permute-start(bf16[16,16,512]{2,1,0:T(8,128)(2,1)S(1)} %broadcast_select_fusion.1), channel_id=1, source_target_pairs={{0,16},{4,20},{8,24},{12,28},{16,32},{20,36},{24,40},{28,44},{32,4... | collective-permute-start | bytes 786440 | tf_op jit(solution)/shard_map/ppermute | solution.py:14
  472.3 10.7 %collective-permute-start.3 = (bf16[16,16,512]{2,1,0:T(8,128)(2,1)S(1)}, bf16[16,16,512]{2,1,0:T(8,128)(2,1)S(1)}, u32[]{:S(2)}, u32[]{:S(2)}) collective-permute-start(bf16[16,16,512]{2,1,0:T(8,128)(2,1)S(1)} %broadcast_select_fusion.2), channel_id=1, source_target_pairs={{0,32},{4,36},{8,40},{12,44},{16,48},{20,52},{24,56},{28,60},{32,6... | collective-permute-start | bytes 786440 | tf_op jit(solution)/shard_map/ppermute | solution.py:14
Sparse Core Ops, SparseCore 0:
  12.5 130.1 all-gather.3
  147.1 134.3 all-gather.5
  285.9 133.5 all-gather.7
  424.1 29.3 reduce-scatter.1
where the time goes:
time: 493 us; the launch traced here: 490 us
  waiting for transfers between devices  440 us (89%)
  matrix products  14.7 us (3%)
  between operations  14.1 us (3%)
  starting transfers between devices  8.78 us (2%)
  local copies, waits for them, and re-layouts  7.76 us (2%)
  other arithmetic  5.18 us (1%)
    all_gather x1, waiting for transfers between devices, on_device(): query_all = add_rows(lax.all_gather(w_query, 'req', axis=0, tiled=True))  134 us
    all_gather x1, waiting for transfers between devices, on_device(): lax.all_gather(w_out, 'req', axis=1, tiled=True)  129 us
    all_gather x1, waiting for transfers between devices, on_device(): keyval = add_rows(lax.all_gather(w_kv, 'req', axis=0, tiled=True))  125 us
    ppermute x4, waiting for transfers between devices, from_behind(): return lax.ppermute(value, axis, pairs)  49.9 us
  transfers between devices with their start and end apart: 8, of which 7 were waited for; matrix products, arithmetic and copies ran while one was open for 5% of the time, Pallas kernels for 0%

commit v1 on v0

--- a/solution.py
+++ b/solution.py
@@ -1,11 +1,125 @@
 import jax
 import jax.numpy as jnp
 from jax import lax
+from jax.experimental import pallas as pl
+from jax.experimental.pallas import tpu as pltpu
 from jax.sharding import PartitionSpec as P
 
 HD = 128
 EXPERTS = 4
 BITS = 4
+MESH = pl.DeviceIdType.MESH
+RING = 8
+PAIR = 2
+
+
+def place(z, x, y):
+    return {"req": ((z + RING) % RING * PAIR + x) * RING + (y + RING) % RING}
+
+
+def gather_kernel(shard_ref, full_ref, local_sem, swap_sems, send_sems, recv_sems):
+    me = lax.axis_index("req")
+    z, x, y = me // (PAIR * RING), me // RING % PAIR, me % RING
+    partner = place(z, 1 - x, y)
+    around = {
+        ("z", 1): place(z + 1, x, y),
+        ("z", -1): place(z - 1, x, y),
+        ("y", 1): place(z, x, y + 1),
+        ("y", -1): place(z, x, y - 1),
+    }
+    barrier = pltpu.get_barrier_semaphore()
+    for device in [partner] + list(around.values()):
+        pl.semaphore_signal(barrier, inc=1, device_id=device, device_id_type=MESH)
+    pl.semaphore_wait(barrier, 5)
+
+    keep = pltpu.make_async_copy(shard_ref, full_ref.at[z, x, y], local_sem)
+    keep.start()
+    swap = pltpu.make_async_remote_copy(
+        src_ref=shard_ref,
+        dst_ref=full_ref.at[z, x, y],
+        send_sem=swap_sems.at[0],
+        recv_sem=swap_sems.at[1],
+        device_id=partner,
+        device_id_type=MESH,
+    )
+    swap.start()
+
+    issued = []
+
+    def send(axis, way, block):
+        slot = len(issued)
+        copy = pltpu.make_async_remote_copy(
+            src_ref=block,
+            dst_ref=block,
+            send_sem=send_sems.at[slot],
+            recv_sem=recv_sems.at[slot],
+            device_id=around[axis, way],
+            device_id_type=MESH,
+        )
+        copy.start()
+        issued.append(copy)
+        return copy
+
+    half = RING // 2
+
+    def one(axis, way, step, _):
+        back = (-way) * step + RING
+        if axis == "z":
+            return full_ref.at[(z + back) % RING, 0, y]
+        return full_ref.at[z, 1, (y + back) % RING]
+
+    def many(axis, way, step, chunk):
+        back = (-way) * step + RING
+        if axis == "y":
+            return full_ref.at[pl.ds(half * chunk, half), 0, (y + back) % RING]
+        return full_ref.at[(z + back) % RING, 1, pl.ds(half * chunk, half)]
+
+    def rounds(block, lanes):
+        flying = {}
+        for step in range(half):
+            for lane in lanes:
+                axis, way, chunk, hops = lane
+                if step < hops:
+                    if step > 0:
+                        flying[lane].wait_recv()
+                    flying[lane] = send(axis, way, block(axis, way, step, chunk))
+        for lane in lanes:
+            flying[lane].wait_recv()
+
+    keep.wait()
+    swap.wait()
+    rounds(one, [(axis, way, 0, half if way == 1 else half - 1) for way in (1, -1) for axis in ("z", "y")])
+    rounds(
+        many,
+        [
+            (axis, way, chunk, half if (way == 1) == (chunk == 0) else half - 1)
+            for chunk in (0, 1)
+            for way in (1, -1)
+            for axis in ("z", "y")
+        ],
+    )
+    for copy in issued:
+        copy.wait_send()
+
+
+def gather_all(shard):
+    rows, columns = shard.shape
+    sends = 4 * RING + 4 * (RING // 2) - 6
+    full = pl.pallas_call(
+        gather_kernel,
+        out_shape=jax.ShapeDtypeStruct((RING, PAIR, RING, rows, columns), shard.dtype),
+        in_specs=[pl.BlockSpec(memory_space=pl.ANY)],
+        out_specs=pl.BlockSpec(memory_space=pl.ANY),
+        scratch_shapes=[
+            pltpu.SemaphoreType.DMA,
+            pltpu.SemaphoreType.DMA((2,)),
+            pltpu.SemaphoreType.DMA((sends,)),
+            pltpu.SemaphoreType.DMA((sends,)),
+        ],
+        compiler_params=pltpu.CompilerParams(collective_id=0, has_side_effects=True),
+        name="gather_weights",
+    )(shard)
+    return full.reshape(RING * PAIR * RING * rows, columns)
 
 
 def from_behind(value, axis, steps):
@@ -70,11 +184,14 @@
     pad_float = padding.astype(jnp.float32)
     local_heads = w_kv.shape[1] // (2 * HD)
 
+    weights = gather_all(jnp.concatenate([w_kv, w_query, w_out.T], axis=1))
+    kv_columns, query_columns = w_kv.shape[1], w_query.shape[1]
+
     def add_rows(piece):
         return jnp.dot(normed, piece, preferred_element_type=jnp.float32)
 
-    keyval = add_rows(lax.all_gather(w_kv, "req", axis=0, tiled=True))
-    query_all = add_rows(lax.all_gather(w_query, "req", axis=0, tiled=True))
+    keyval = add_rows(weights[:, :kv_columns])
+    query_all = add_rows(weights[:, kv_columns : kv_columns + query_columns])
     keyval = keyval.reshape(count, local_heads, 2, HD)
     keys_rot = rotate(keyval[:, :, 0, :], position)
     keyval = (
@@ -95,8 +212,11 @@
         * pad_float[:, None, None, None]
     )
     mixed = mixed.reshape(count, local_heads * EXPERTS * HD).astype(jnp.bfloat16)
-    partial_out = jnp.dot(
-        mixed, lax.all_gather(w_out, "req", axis=1, tiled=True), preferred_element_type=jnp.float32
+    partial_out = lax.dot_general(
+        mixed,
+        weights[:, kv_columns + query_columns :],
+        (((1,), (1,)), ((), ())),
+        preferred_element_type=jnp.float32,
     )
     attended = lax.psum_scatter(
         partial_out.astype(jnp.bfloat16), "tensor", scatter_dimension=1, tiled=True

time: 493 us -> 196 us (0.40)
  the two profiles are of different devices: /device:TPU:1 before, /device:TPU:2 now
where the time goes in v1:
time: 196 us; the launch traced here: 195 us
  Pallas kernels  84.6 us (43%)
  waiting for transfers between devices  57.4 us (29%)
  matrix products  15.5 us (8%)
  between operations  14.4 us (7%)
  local copies, waits for them, and re-layouts  8.22 us (4%)
  starting transfers between devices  7.72 us (4%)
  other arithmetic  7.22 us (4%)
    pallas_call x1, Pallas kernels, gather_all(): pl.pallas_call(gather_kernel, out_shape=jax.ShapeDtypeStruct((RING, PAIR,...  84.6 us
    ppermute x4, waiting for transfers between devices, from_behind(): return lax.ppermute(value, axis, pairs)  57.4 us
    ppermute x4, starting transfers between devices, from_behind(): return lax.ppermute(value, axis, pairs)  7.68 us
    dot_general x2, matrix products, add_rows(): return jnp.dot(normed, piece, preferred_element_type=jnp.float32)  6.66 us
    dot_general x1, matrix products, on_device(): lax.dot_general(mixed, weights[:, kv_columns + query_columns:], (((1,), (...  4.45 us
  transfers between devices with their start and end apart: 5, of which 4 were waited for; matrix products, arithmetic and copies ran while one was open for 1% of the time, Pallas kernels for 0%

profile of v1, /device:TPU:2, one launch (start us, length us, event | category | flops | bytes accessed | tf_op | source)
XLA Modules:
  0.0 195.2 jit_solution(18285212794364480131)
XLA Ops:
  7.2 1.5 fusion.8
  8.8 1.4 pad_maximum_fusion.1.shard_ref
  10.2 84.6 %gather_weights.1 = bf16[8,2,8,16,2560]{4,3,2,1,0:T(8,128)(2,1)} custom-call(bf16[16,2560]{1,0:T(8,128)(2,1)} %pad_maximum_fusion.1.shard_ref), custom_call_target="tpu_custom_call" | custom-call | tf_op jit(solution)/shard_map/gather_weights/pallas_call | solution.py:108
  94.9 3.5 %fusion.3 = f32[256,1024]{1,0:T(8,128)S(1)} fusion(bf16[2048,2560]{1,0:T(8,128)(2,1)} %bitcast.59, bf16[256,2048]{1,0:T(8,128)(2,1)S(1)} %copy-done.3, f32[2048]{0:T(1024)S(1)} %copy-done.6, f32[256]{0:T(256)S(1)} %add_rsqrt_fusion), kind=kOutput, calls=%fused_computation.5 | convolution fusion | flops 1075838976 | bytes 6300672 | tf_op jit(solution)/shard_map/dot_general | solution.py:191
  98.4 3.2 %fusion.11 = f32[256,512]{1,0:T(8,128)} fusion(bf16[2048,2560]{1,0:T(8,128)(2,1)} %bitcast.60, bf16[256,2048]{1,0:T(8,128)(2,1)S(1)} %copy-done.3, f32[2048]{0:T(1024)S(1)} %copy-done.6, f32[256]{0:T(256)S(1)} %add_rsqrt_fusion), kind=kOutput, calls=%fused_computation.13 | convolution fusion | flops 538968064 | bytes 3679232 | tf_op jit(solution)/shard_map/dot_general | solution.py:191
  101.8 2.1 %gather_fusion = s32[256]{0:T(256)S(1)} fusion(s32[256]{0:T(256)S(1)} %bitcast.58, s32[1024]{0:T(1024)S(1)} %pad_clamp_fusion), kind=kCustom, calls=%fused_computation | custom fusion | bytes 3072 | tf_op jit(solution)/shard_map/gather | solution.py:146
  103.9 1.9 gather_fusion.1
  106.0 0.5 reshape.224
  106.5 1.4 reshape.223
  107.9 0.4 fusion.55
  108.4 0.5 multiply_cosine_fusion
  108.9 0.9 multiply_subtract_fusion
  110.2 1.2 convolution_convert_fusion
  111.6 0.6 fusion.56
  112.2 0.3 fusion.17
  112.5 0.5 fusion.24
  113.1 0.9 fusion.31
  114.1 0.4 fusion.21
  114.7 1.4 fusion.19
  116.1 0.4 convert_element_type.56
  116.5 4.5 %fusion.5 = bf16[256,2048]{1,0:T(8,128)(2,1)} fusion(bf16[256,1024]{1,0:T(8,128)(2,1)S(1)} %convert_element_type.56, bf16[2048,2560]{1,0:T(8,128)(2,1)} %bitcast.61), kind=kOutput, calls=%fused_computation.9 | convolution fusion | flops 1074266112 | bytes 5767168 | tf_op jit(solution)/shard_map/dot_general | solution.py:215
  121.1 0.4 copy.34
  121.5 0.4 stack.10
  122.0 1.9 collective-permute-start
  124.0 13.6 %collective-permute-done = bf16[16,16,512]{2,1,0:T(8,128)(2,1)S(1)} collective-permute-done((bf16[16,16,512]{2,1,0:T(8,128)(2,1)S(1)}, bf16[16,16,512]{2,1,0:T(8,128)(2,1)S(1)}, u32[]{:S(2)}, u32[]{:S(2)}) %collective-permute-start) | collective-permute-done | bytes 262176 | tf_op jit(solution)/shard_map/ppermute | solution.py:128
  137.8 1.9 collective-permute-start.1
  139.7 19.1 %collective-permute-done.1 = bf16[16,16,512]{2,1,0:T(8,128)(2,1)S(1)} collective-permute-done((bf16[16,16,512]{2,1,0:T(8,128)(2,1)S(1)}, bf16[16,16,512]{2,1,0:T(8,128)(2,1)S(1)}, u32[]{:S(2)}, u32[]{:S(2)}) %collective-permute-start.1) | collective-permute-done | bytes 262176 | tf_op jit(solution)/shard_map/ppermute | solution.py:128
  158.9 1.9 collective-permute-start.2
  160.8 14.8 %collective-permute-done.2 = bf16[16,16,512]{2,1,0:T(8,128)(2,1)S(1)} collective-permute-done((bf16[16,16,512]{2,1,0:T(8,128)(2,1)S(1)}, bf16[16,16,512]{2,1,0:T(8,128)(2,1)S(1)}, u32[]{:S(2)}, u32[]{:S(2)}) %collective-permute-start.2) | collective-permute-done | bytes 262176 | tf_op jit(solution)/shard_map/ppermute | solution.py:128
  175.6 1.9 collective-permute-start.3
  177.6 10.0 %collective-permute-done.3 = bf16[16,16,512]{2,1,0:T(8,128)(2,1)S(1)} collective-permute-done((bf16[16,16,512]{2,1,0:T(8,128)(2,1)S(1)}, bf16[16,16,512]{2,1,0:T(8,128)(2,1)S(1)}, u32[]{:S(2)}, u32[]{:S(2)}) %collective-permute-start.3) | collective-permute-done | bytes 262176 | tf_op jit(solution)/shard_map/ppermute | solution.py:128
  187.5 0.8 broadcast_select_fusion.3
  (41 shorter events, 2.0 us)
Async XLA Ops:
  7.2 105.3 %copy-start = (f32[2048,4]{0,1:T(4,128)S(1)}, f32[2048,4]{0,1:T(4,128)}, u32[]{:S(2)}) copy-start(f32[2048,4]{0,1:T(4,128)} %param.15) | copy-start | bytes 98308
  7.2 181.1 %reduce-scatter.2.cloned.1.call-start = ((), (), s32[]{:S(2)}) async-start(), calls=%async_computation.1 | async-start | bytes 1310720 | tf_op jit(solution)/shard_map/reduce_scatter | solution.py:221
  10.2 84.7 %copy-start.3 = (bf16[256,2048]{1,0:T(8,128)(2,1)S(1)}, bf16[256,2048]{1,0:T(8,128)(2,1)}, u32[]{:S(2)}) copy-start(bf16[256,2048]{1,0:T(8,128)(2,1)} %param.10) | copy-start | bytes 3145732
  10.2 84.7 %copy-start.6 = (f32[2048]{0:T(1024)S(1)}, f32[2048]{0:T(1024)}, u32[]{:S(2)}) copy-start(f32[2048]{0:T(1024)} %param.14) | copy-start | bytes 24580
  98.3 3.2 %copy-start.1 = (s32[1,256]{1,0:T(1,128)S(1)}, s32[1,256]{1,0:T(1,128)}, u32[]{:S(2)}) copy-start(s32[1,256]{1,0:T(1,128)} %param.11) | copy-start | bytes 3076
  98.4 5.5 %copy-start.2 = (s32[256]{0:T(256)S(1)}, s32[256]{0:T(256)}, u32[]{:S(2)}) copy-start(s32[256]{0:T(256)} %param.12) | copy-start | bytes 3076
  101.6 4.3 %copy-start.4 = (s32[256,2]{0,1:T(2,128)S(1)}, s32[256,2]{0,1:T(2,128)}, u32[]{:S(2)}) copy-start(s32[256,2]{0,1:T(2,128)} %param.13) | copy-start | bytes 6148
  121.0 3.0 %copy-start.5 = (s32[16]{0:T(128)S(1)}, s32[16]{0:T(128)}, u32[]{:S(2)}) copy-start(s32[16]{0:T(128)} %param.19) | copy-start | bytes 196
  122.0 15.6 %collective-permute-start = (bf16[16,16,512]{2,1,0:T(8,128)(2,1)S(1)}, bf16[16,16,512]{2,1,0:T(8,128)(2,1)S(1)}, u32[]{:S(2)}, u32[]{:S(2)}) collective-permute-start(bf16[16,16,512]{2,1,0:T(8,128)(2,1)S(1)} %multiply_convert_fusion), channel_id=1, source_target_pairs={{0,4},{4,8},{8,12},{12,16},{16,20},{20,24},{24,28},{28,32},{32,36}... | collective-permute-start | bytes 786440 | tf_op jit(solution)/shard_map/ppermute | solution.py:128
  137.8 21.0 %collective-permute-start.1 = (bf16[16,16,512]{2,1,0:T(8,128)(2,1)S(1)}, bf16[16,16,512]{2,1,0:T(8,128)(2,1)S(1)}, u32[]{:S(2)}, u32[]{:S(2)}) collective-permute-start(bf16[16,16,512]{2,1,0:T(8,128)(2,1)S(1)} %broadcast_select_fusion), channel_id=1, source_target_pairs={{0,8},{4,12},{8,16},{12,20},{16,24},{20,28},{24,32},{28,36},{32,40... | collective-permute-start | bytes 786440 | tf_op jit(solution)/shard_map/ppermute | solution.py:128
  158.9 16.7 %collective-permute-start.2 = (bf16[16,16,512]{2,1,0:T(8,128)(2,1)S(1)}, bf16[16,16,512]{2,1,0:T(8,128)(2,1)S(1)}, u32[]{:S(2)}, u32[]{:S(2)}) collective-permute-start(bf16[16,16,512]{2,1,0:T(8,128)(2,1)S(1)} %broadcast_select_fusion.1), channel_id=1, source_target_pairs={{0,16},{4,20},{8,24},{12,28},{16,32},{20,36},{24,40},{28,44},{32,4... | collective-permute-start | bytes 786440 | tf_op jit(solution)/shard_map/ppermute | solution.py:128
  175.6 11.9 %collective-permute-start.3 = (bf16[16,16,512]{2,1,0:T(8,128)(2,1)S(1)}, bf16[16,16,512]{2,1,0:T(8,128)(2,1)S(1)}, u32[]{:S(2)}, u32[]{:S(2)}) collective-permute-start(bf16[16,16,512]{2,1,0:T(8,128)(2,1)S(1)} %broadcast_select_fusion.2), channel_id=1, source_target_pairs={{0,32},{4,36},{8,40},{12,44},{16,48},{20,52},{24,56},{28,60},{32,6... | collective-permute-start | bytes 786440 | tf_op jit(solution)/shard_map/ppermute | solution.py:128
Sparse Core Ops, SparseCore 0:
  121.1 24.2 reduce-scatter.1

commit v2 on v0

v2 whole, which is shorter than its diff:
```python
import functools

import jax
import jax.numpy as jnp
from jax import lax
from jax.experimental import pallas as pl
from jax.experimental.pallas import tpu as pltpu
from jax.sharding import PartitionSpec as P

HD = 128
EXPERTS = 4
SLOTS = 2
BITS = 4
MESH = pl.DeviceIdType.MESH
RING = 8
PAIR = 2
CORES = 2
HALF = RING // 2
REQ = RING * PAIR * RING
F32 = jnp.float32
BF16 = jnp.bfloat16


def place(z, x, y):
    return {"req": ((z + RING) % RING * PAIR + x) * RING + (y + RING) % RING}


def layer_kernel(
    parts,
    heads,
    tokens_ref,
    gain_ref,
    router_ref,
    cols_ref,
    rows_ref,
    cos_ref,
    sin_ref,
    shard_ref,
    attended_ref,
    cache_ref,
    full_ref,
    normed_ref,
    bias_ref,
    gates_ref,
    stages_ref,
    inbox_ref,
    query_ref,
    mixed_ref,
    pair_out_ref,
    pair_in_ref,
    far_out_ref,
    far_in_ref,
    local_sem,
    swap_sems,
    send_sems,
    recv_sems,
    page_sems,
    reduce_sems,
):
    count = tokens_ref.shape[0]
    me = lax.axis_index("req")
    z, x, y = me // (PAIR * RING), me // RING % PAIR, me % RING
    mine = lax.axis_index("tensor")
    low, core = mine // CORES, mine % CORES
    partner = place(z, 1 - x, y)
    core_mate = {"tensor": low * CORES + (1 - core)}
    far_mate = {"tensor": (1 - low) * CORES + core}
    around = {
        ("z", 1): place(z + 1, x, y),
        ("z", -1): place(z - 1, x, y),
        ("y", 1): place(z, x, y + 1),
        ("y", -1): place(z, x, y - 1),
    }
    levels = [2**level for level in reversed(range(BITS))]
    ahead = [{"req": (me + shift) % REQ} for shift in levels]
    behind = [{"req": (me + REQ - shift) % REQ} for shift in levels]

    barrier = pltpu.get_barrier_semaphore()
    greeted = [partner, core_mate, far_mate] + list(around.values()) + ahead + behind
    for device in greeted:
        pl.semaphore_signal(barrier, inc=1, device_id=device, device_id_type=MESH)
    pl.semaphore_wait(barrier, len(greeted))

    def remote(src, dst, send_sem, recv_sem, device):
        copy = pltpu.make_async_remote_copy(
            src_ref=src,
            dst_ref=dst,
            send_sem=send_sem,
            recv_sem=recv_sem,
            device_id=device,
            device_id_type=MESH,
        )
        copy.start()
        return copy

    keep = pltpu.make_async_copy(shard_ref, full_ref.at[z, x, y], local_sem)
    keep.start()
    swap = remote(shard_ref, full_ref.at[z, x, y], swap_sems.at[0], swap_sems.at[1], partner)
    issued = []

    def send(axis, way, block):
        slot = len(issued)
        copy = remote(block, block, send_sems.at[slot], recv_sems.at[slot], around[axis, way])
        issued.append(copy)
        return copy

    def single(axis, way, step):
        back = (-way) * step + RING
        if axis == "z":
            return full_ref.at[(z + back) % RING, 0, y]
        return full_ref.at[z, 1, (y + back) % RING]

    def several(axis, way, step, part, chunk):
        back = (-way) * step + RING
        columns = pl.ds(*parts[part])
        run = pl.ds(HALF * chunk, HALF)
        if axis == "y":
            return full_ref.at[run, 0, (y + back) % RING, :, columns]
        return full_ref.at[(z + back) % RING, 1, run, :, columns]

    flying = {}
    streams = [(axis, way) for way in (1, -1) for axis in ("z", "y")]

    def first_round(step):
        for axis, way in streams:
            if step < (HALF if way == 1 else HALF - 1):
                if step > 0:
                    flying[axis, way].wait_recv()
                flying[axis, way] = send(axis, way, single(axis, way, step))

    def first_end():
        for stream in streams:
            flying[stream].wait_recv()

    def turn(part, step, chunk):
        for axis, way in streams:
            if step < (HALF if (way == 1) == (chunk == 0) else HALF - 1):
                lane = (axis, way, part, chunk)
                if step > 0:
                    flying[lane].wait_recv()
                flying[lane] = send(axis, way, several(axis, way, step, part, chunk))

    def arrived(part):
        for chunk in (0, 1):
            for axis, way in streams:
                flying[axis, way, part, chunk].wait_recv()

    def column(index):
        return cols_ref[:, index : index + 1]

    def rotate(values):
        return values * cos_ref[...] + pltpu.roll(values, HD // 2, 1) * sin_ref[...]

    def norm():
        block = 32
        for row in range(0, count, block):
            x_float = tokens_ref[row : row + block, :].astype(F32)
            scale = lax.rsqrt(jnp.mean(x_float * x_float, axis=1, keepdims=True) + 1e-06)
            normed_ref[row : row + block, :] = (x_float * scale * gain_ref[...]).astype(BF16)

    def route():
        logits = jnp.dot(normed_ref[...], router_ref[...], preferred_element_type=F32)
        for slot in range(SLOTS):
            expert = column(2 + slot)
            logit = jnp.zeros((count, 1), F32)
            for index in range(EXPERTS):
                logit = logit + jnp.where(expert == index, logits[:, index : index + 1], 0.0)
            gate = 1.0 / (1.0 + jnp.exp(-logit))
            gates_ref[slot] = jnp.broadcast_to(gate * column(1).astype(F32), (count, HD))

    def mask():
        query_index = lax.broadcasted_iota(jnp.int32, (count, count), 0)
        key_index = lax.broadcasted_iota(jnp.int32, (count, count), 1)
        same = (column(0) == rows_ref[0:1, :]) & (key_index <= query_index)
        allowed = same & ((rows_ref[1:2, :] == 1) | (key_index == query_index))
        bias_ref[...] = jnp.where(allowed, 0.0, -1e30)

    def weights_of(first, size):
        block = full_ref[:, :, :, :, first : first + size]
        return block.reshape(REQ * block.shape[3], size)

    def project_keys():
        first, size = parts[0]
        keyval = jnp.dot(normed_ref[...], weights_of(first, size), preferred_element_type=F32)
        padded = column(1).astype(F32)
        for head in range(heads):
            at = head * 2 * HD
            stages_ref[0, :, at : at + HD] = (rotate(keyval[:, at : at + HD]) * padded).astype(BF16)
            stages_ref[0, :, at + HD : at + 2 * HD] = (
                keyval[:, at + HD : at + 2 * HD] * padded
            ).astype(BF16)

    moves = []

    def page_send(level):
        moves.append(
            remote(
                stages_ref.at[level],
                inbox_ref.at[level],
                page_sems.at[0, level],
                page_sems.at[1, level],
                ahead[level],
            )
        )

    def page_take(level):
        moves[level].wait_recv()
        taken = column(4) // levels[level] % 2 == 1
        chosen = jnp.where(
            taken, inbox_ref[level].astype(F32), stages_ref[level].astype(F32)
        ).astype(BF16)
        if level == BITS - 1:
            cache_ref[...] = chosen
        else:
            stages_ref[level + 1] = chosen

    def project_queries(head):
        size = EXPERTS * HD
        every = jnp.dot(
            normed_ref[...], weights_of(parts[1][0] + head * size, size), preferred_element_type=F32
        )
        for slot in range(SLOTS):
            expert = column(2 + slot)
            chosen = jnp.zeros((count, HD), F32)
            for index in range(EXPERTS):
                chosen = chosen + jnp.where(
                    expert == index, every[:, index * HD : (index + 1) * HD], 0.0
                )
            query_ref[head * SLOTS + slot] = rotate(chosen).astype(BF16)

    def attend(head):
        at = head * 2 * HD
        keys = stages_ref[0, :, at : at + HD]
        values = stages_ref[0, :, at + HD : at + 2 * HD]
        outs = []
        for slot in range(SLOTS):
            scores = lax.dot_general(
                query_ref[head * SLOTS + slot],
                keys,
                (((1,), (1,)), ((), ())),
                preferred_element_type=F32,
            )
            masked = scores * (HD**-0.5) + bias_ref[...]
            weights = jnp.exp(masked - jnp.max(masked, axis=1, keepdims=True))
            total = jnp.sum(weights, axis=1, keepdims=True)
            summed = jnp.dot(weights.astype(BF16), values, preferred_element_type=F32)
            outs.append(summed / total * gates_ref[slot])
        for index in range(EXPERTS):
            mix = jnp.zeros((count, HD), F32)
            for slot in range(SLOTS):
                mix = mix + jnp.where(column(2 + slot) == index, outs[slot], 0.0)
            first = (head * EXPERTS + index) * HD
            mixed_ref[:, first : first + HD] = mix.astype(BF16)

    def project_out(owner):
        span = RING // (PAIR * CORES)
        first, size = parts[2]
        block = full_ref[pl.ds(owner * span, span), :, :, :, first : first + size]
        return lax.dot_general(
            mixed_ref[...],
            block.reshape(span * PAIR * RING * block.shape[3], size),
            (((1,), (1,)), ((), ())),
            preferred_element_type=F32,
        )

    norm()
    keep.wait()
    swap.wait()
    first_round(0)
    mask()
    first_round(1)
    route()
    for step in (2, 3):
        first_round(step)
    first_end()
    for step in range(HALF):
        for chunk in (0, 1):
            turn(0, step, chunk)
    turn(1, 0, 0)
    turn(1, 0, 1)
    arrived(0)
    project_keys()
    page_send(0)
    for step in range(1, HALF):
        for chunk in (0, 1):
            turn(1, step, chunk)
    page_take(0)
    page_send(1)
    turn(2, 0, 0)
    turn(2, 0, 1)
    arrived(1)
    project_queries(0)
    turn(2, 1, 0)
    project_queries(1)
    turn(2, 1, 1)
    page_take(1)
    page_send(2)
    turn(2, 2, 0)
    attend(0)
    turn(2, 2, 1)
    attend(1)
    turn(2, 3, 0)
    turn(2, 3, 1)
    page_take(2)
    page_send(3)
    arrived(2)

    def pair_send(index, owner):
        pair_out_ref[index] = project_out(owner).astype(BF16)
        return remote(
            pair_out_ref.at[index],
            pair_in_ref.at[index],
            reduce_sems.at[0, index],
            reduce_sems.at[1, index],
            core_mate,
        )

    pairs = [pair_send(0, (1 - low) * CORES + (1 - core))]
    far = project_out((1 - low) * CORES + core)
    pairs[0].wait_recv()
    far_out_ref[...] = (far + pair_in_ref[0].astype(F32)).astype(BF16)
    far_copy = remote(far_out_ref, far_in_ref, reduce_sems.at[0, 2], reduce_sems.at[1, 2], far_mate)
    pairs.append(pair_send(1, low * CORES + (1 - core)))
    near = project_out(low * CORES + core)
    pairs[1].wait_recv()
    near = near + pair_in_ref[1].astype(F32)
    page_take(3)
    far_copy.wait_recv()
    attended_ref[...] = (near + far_in_ref[...].astype(F32)).astype(BF16)

    for copy in issued + moves + pairs + [far_copy]:
        copy.wait_send()


def on_device(
    tokens, segment_ids, padding, attn_experts, gain, w_router, w_query, w_kv, w_out, page_shift
):
    count, width = tokens.shape
    seg_row = segment_ids[0]
    starts = jnp.sum((seg_row[None, :] < seg_row[:, None]).astype(jnp.int32), axis=1)
    position = jnp.arange(count, dtype=jnp.int32) - starts
    half_size = HD // 2
    freqs = 10000.0 ** (-jnp.arange(half_size, dtype=F32) / half_size)
    angles = position.astype(F32)[:, None] * freqs[None, :]
    cosine, sine = jnp.cos(angles), jnp.sin(angles)
    cosine = jnp.concatenate([cosine, cosine], axis=1)
    sine = jnp.concatenate([-sine, sine], axis=1)
    shifts = jnp.repeat(page_shift, count // page_shift.shape[0])
    cols = jnp.stack([seg_row, padding, attn_experts[:, 0], attn_experts[:, 1], shifts], axis=1)
    rows = jnp.stack([seg_row, padding], axis=0)
    router = jnp.pad(w_router, ((0, 0), (0, HD - EXPERTS))).astype(BF16)
    shard = jnp.concatenate([w_kv, w_query, w_out.T], axis=1)
    kv_size, query_size, out_size = w_kv.shape[1], w_query.shape[1], w_out.shape[0]
    parts = ((0, kv_size), (kv_size, query_size), (kv_size + query_size, out_size))
    heads = kv_size // (2 * HD)
    slab = width // (PAIR * CORES)
    sends = (4 * HALF - 2) + 3 * (8 * HALF - 4)
    vmem = pl.BlockSpec(memory_space=pltpu.VMEM)
    attended, cache = pl.pallas_call(
        functools.partial(layer_kernel, parts, heads),
        out_shape=(
            jax.ShapeDtypeStruct((count, slab), BF16),
            jax.ShapeDtypeStruct((count, kv_size), BF16),
        ),
        in_specs=[vmem] * 7 + [pl.BlockSpec(memory_space=pl.ANY)],
        out_specs=(vmem, vmem),
        scratch_shapes=[
            pltpu.VMEM((RING, PAIR, RING) + shard.shape, BF16),
            pltpu.VMEM((count, width), BF16),
            pltpu.VMEM((count, count), F32),
            pltpu.VMEM((SLOTS, count, HD), F32),
            pltpu.VMEM((BITS, count, kv_size), BF16),
            pltpu.VMEM((BITS, count, kv_size), BF16),
            pltpu.VMEM((heads * SLOTS, count, HD), BF16),
            pltpu.VMEM((count, heads * EXPERTS * HD), BF16),
            pltpu.VMEM((2, count, slab), BF16),
            pltpu.VMEM((2, count, slab), BF16),
            pltpu.VMEM((count, slab), BF16),
            pltpu.VMEM((count, slab), BF16),
            pltpu.SemaphoreType.DMA,
            pltpu.SemaphoreType.DMA((2,)),
            pltpu.SemaphoreType.DMA((sends,)),
            pltpu.SemaphoreType.DMA((sends,)),
            pltpu.SemaphoreType.DMA((2, BITS)),
            pltpu.SemaphoreType.DMA((2, 3)),
        ],
        compiler_params=pltpu.CompilerParams(collective_id=0, has_side_effects=True),
        name="layer",
    )(tokens, gain[None, :], router, cols, rows, cosine, sine, shard)
    pages = page_shift.shape[0]
    return attended, cache.reshape(pages, count // pages, kv_size)


def solution(mesh):
    placed = (
        P("req", None),
        P("req", None),
        P("req"),
        P("req", None),
        P(),
        P(),
        P("req", "tensor"),
        P("req", "tensor"),
        P("tensor", "req"),
        P(),
    )
    return jax.shard_map(
        on_device,
        mesh=mesh,
        in_specs=placed,
        out_specs=(P("req", "tensor"), P("req", None, "tensor")),
        check_vma=False,
    )
```

time: 493 us -> 142 us (0.29)
  waiting for transfers between devices: 440 us -> 0 us
  Pallas kernels: 0 us -> 128 us
  matrix products: 14.7 us -> 0 us
  between operations: 14.1 us -> 0.72 us
  starting transfers between devices: 8.78 us -> 0 us
    all_gather x3 -> x0, waiting for transfers between devices: 388 us -> none  [the longest x1 134 us: on_device(): query_all = add_rows(lax.all_gather(w_query, 'req', axis=0, tiled=True))]
    pallas_call x0 -> x1, Pallas kernels: none -> 128 us  [on_device(): pl.pallas_call(functools.partial(layer_kernel, parts, heads), out_shape=(...]
    ppermute x4 -> x0, waiting for transfers between devices: 49.9 us -> none  [from_behind(): return lax.ppermute(value, axis, pairs)]
    dot_general x8 -> x0, matrix products: 14.1 us -> none  [the longest x2 5.81 us: add_rows(): return jnp.dot(normed, piece, preferred_element_type=jnp.float32)]
    ppermute x4 -> x0, starting transfers between devices: 8.63 us -> none  [from_behind(): return lax.ppermute(value, axis, pairs)]
  transfers between devices with their start and end apart: 8 -> 0, of which waited for: 7 -> 0; matrix products, arithmetic and copies ran while one was open for 5% -> 0% of each run, Pallas kernels for 0% -> 0%
where the time goes in v2:
time: 142 us; the launch traced here: 139 us
  Pallas kernels  128 us (90%)
  local copies, waits for them, and re-layouts  6 us (4%)
  other arithmetic  4.97 us (4%)
    pallas_call x1, Pallas kernels, on_device(): pl.pallas_call(functools.partial(layer_kernel, parts, heads), out_shape=(...  128 us
    unnamed x16, local copies, waits for them, and re-layouts  3.15 us

profile of v2, /device:TPU:1, one launch (start us, length us, event | category | flops | bytes accessed | tf_op | source)
XLA Modules:
  0.0 139.5 jit_solution(757021547522089243)
XLA Ops:
  0.6 0.0 copy-start.3
  0.7 0.9 convert_reduce_fusion
  1.6 1.3 pad_add_fusion.1.rows_ref
  2.9 0.0 copy-start.4
  2.9 0.0 copy-start.5
  2.9 0.0 copy-start.6
  2.9 0.8 broadcast_in_dim.9
  3.7 0.0 copy-start.2
  3.7 0.1 stack_reshape.3
  3.7 0.0 copy-done.4
  3.7 0.0 copy-done.5
  3.7 0.0 copy-done.6
  3.8 0.0 copy-start.1
  3.8 0.0 copy-done.3
  3.8 0.6 copy-done.2
  4.4 0.1 copy-done.1
  4.5 1.3 pad_maximum_fusion.2.shard_ref
  5.9 0.8 copy.24.cols_ref
  6.7 0.5 fusion
  7.2 0.8 pad_maximum_fusion
  8.0 0.3 copy.23
  8.4 0.9 pad.5.router_ref
  9.3 127.8 %layer.1 = (bf16[256,512]{1,0:T(8,128)(2,1)}, bf16[256,512]{1,0:T(8,128)(2,1)}) custom-call(bf16[256,2048]{1,0:T(8,128)(2,1)} %tokens_ref.1, f32[1,2048]{1,0:T(1,128)} %bitcast.11, bf16[2048,128]{1,0:T(8,128)(2,1)} %pad.5.router_ref, s32[256,5]{1,0:T(8,128)} %copy.24.cols_ref, s32[2,256]{1,0:T(2,128)} %pad_add_fusion.1.rows_ref, ...), custom_call_target="tpu_custom_call" | custom-call | tf_op jit(solution)/shard_map/layer/pallas_call | solution.py:359
  137.0 0.0 copy-start
  137.1 1.7 %copy.27 = bf16[256,512]{1,0:T(8,128)(2,1)} copy(bf16[256,512]{1,0:T(8,128)(2,1)} %get-tuple-element.13) | data formatting | bytes 524288
  138.8 0.0 copy-done
  138.8 0.7 copy.28
  (4 shorter events, 0.0 us)
Async XLA Ops:
  0.6 3.2 %copy-start.3 = (f32[2048,4]{0,1:T(4,128)S(1)}, f32[2048,4]{0,1:T(4,128)}, u32[]{:S(2)}) copy-start(f32[2048,4]{0,1:T(4,128)} %param.15) | copy-start | bytes 98308
  2.9 0.9 copy-start.4
  2.9 0.9 copy-start.5
  2.9 0.9 copy-start.6
  3.7 0.8 copy-start.2
  3.8 0.8 copy-start.1
  137.0 1.7 %copy-start = (bf16[256,512]{1,0:T(8,128)(2,1)S(1)}, bf16[256,512]{1,0:T(8,128)(2,1)}, u32[]{:S(2)}) copy-start(bf16[256,512]{1,0:T(8,128)(2,1)} %get-tuple-element.5) | copy-start | bytes 786436

commit v3 on v2

--- a/solution.py
+++ b/solution.py
@@ -32,10 +32,13 @@
     gain_ref,
     router_ref,
     cols_ref,
-    rows_ref,
+    seg_ref,
+    pad_ref,
     cos_ref,
     sin_ref,
-    shard_ref,
+    kv_ref,
+    wide_ref,
+    out_ref,
     attended_ref,
     cache_ref,
     full_ref,
@@ -50,7 +53,7 @@
     pair_in_ref,
     far_out_ref,
     far_in_ref,
-    local_sem,
+    keep_sems,
     swap_sems,
     send_sems,
     recv_sems,
@@ -93,57 +96,64 @@
         copy.start()
         return copy
 
-    keep = pltpu.make_async_copy(shard_ref, full_ref.at[z, x, y], local_sem)
-    keep.start()
-    swap = remote(shard_ref, full_ref.at[z, x, y], swap_sems.at[0], swap_sems.at[1], partner)
+    (kv_first, kv_size), (query_first, query_size), (out_first, out_size) = parts
+    begin, rest = pl.ds(0, out_first), pl.ds(out_first, out_size)
+    keeps, swaps = [], []
+    for index, (ref, (first, size)) in enumerate(zip((kv_ref, wide_ref, out_ref), parts)):
+        here = full_ref.at[z, x, y, :, pl.ds(first, size)]
+        swaps.append(remote(ref, here, swap_sems.at[0, index], swap_sems.at[1, index], partner))
+        keep = pltpu.make_async_copy(ref, here, keep_sems.at[index])
+        keep.start()
+        keeps.append(keep)
     issued = []
-
-    def send(axis, way, block):
+    flying = {}
+
+    def send(lane, block):
+        axis, way = lane[0], lane[1]
         slot = len(issued)
         copy = remote(block, block, send_sems.at[slot], recv_sems.at[slot], around[axis, way])
         issued.append(copy)
-        return copy
-
-    def single(axis, way, step):
-        back = (-way) * step + RING
-        if axis == "z":
-            return full_ref.at[(z + back) % RING, 0, y]
-        return full_ref.at[z, 1, (y + back) % RING]
-
-    def several(axis, way, step, part, chunk):
-        back = (-way) * step + RING
-        columns = pl.ds(*parts[part])
+        flying[lane] = copy
+
+    def forward(step, hops, lane, block):
+        if step < hops:
+            if step > 0:
+                flying[lane].wait_recv()
+            send(lane, block)
+
+    def first_round(step):
+        for way in (1, -1):
+            back = (-way) * step + RING
+            hops = HALF if way == 1 else HALF - 1
+            there = (y + back) % RING
+            forward(step, hops, ("y", way, "whole"), full_ref.at[z, 1, there])
+            forward(step, hops, ("z", way, "begin"), full_ref.at[(z + back) % RING, 0, y, :, begin])
+            forward(step, hops, ("y", way, "rest"), full_ref.at[z, 0, there, :, rest])
+
+    def first_turn(step, chunk):
         run = pl.ds(HALF * chunk, HALF)
-        if axis == "y":
-            return full_ref.at[run, 0, (y + back) % RING, :, columns]
-        return full_ref.at[(z + back) % RING, 1, run, :, columns]
-
-    flying = {}
-    streams = [(axis, way) for way in (1, -1) for axis in ("z", "y")]
-
-    def first_round(step):
-        for axis, way in streams:
-            if step < (HALF if way == 1 else HALF - 1):
-                if step > 0:
-                    flying[axis, way].wait_recv()
-                flying[axis, way] = send(axis, way, single(axis, way, step))
-
-    def first_end():
-        for stream in streams:
-            flying[stream].wait_recv()
-
-    def turn(part, step, chunk):
-        for axis, way in streams:
-            if step < (HALF if (way == 1) == (chunk == 0) else HALF - 1):
-                lane = (axis, way, part, chunk)
-                if step > 0:
-                    flying[lane].wait_recv()
-                flying[lane] = send(axis, way, several(axis, way, step, part, chunk))
-
-    def arrived(part):
-        for chunk in (0, 1):
-            for axis, way in streams:
-                flying[axis, way, part, chunk].wait_recv()
+        for way in (1, -1):
+            back = (-way) * step + RING
+            hops = HALF if (way == 1) == (chunk == 0) else HALF - 1
+            forward(step, hops, ("z", way, 0, chunk), full_ref.at[(z + back) % RING, 1, run, :, begin])
+            forward(step, hops, ("y", way, 0, chunk), full_ref.at[run, 0, (y + back) % RING, :, begin])
+
+    def last_turn(step, chunk):
+        run = pl.ds(HALF * (chunk // 2), HALF)
+        for way in (1, -1):
+            back = (-way) * step + RING
+            hops = HALF if (way == 1) == (chunk % 2 == 0) else HALF - 1
+            forward(
+                step,
+                hops,
+                ("z", way, 1, chunk),
+                full_ref.at[(z + back) % RING, chunk % 2, run, :, rest],
+            )
+
+    def arrived(kind):
+        for lane, copy in flying.items():
+            if lane[2] in kind:
+                copy.wait_recv()
 
     def column(index):
         return cols_ref[:, index : index + 1]
@@ -156,23 +166,26 @@
         for row in range(0, count, block):
             x_float = tokens_ref[row : row + block, :].astype(F32)
             scale = lax.rsqrt(jnp.mean(x_float * x_float, axis=1, keepdims=True) + 1e-06)
-            normed_ref[row : row + block, :] = (x_float * scale * gain_ref[...]).astype(BF16)
-
-    def route():
-        logits = jnp.dot(normed_ref[...], router_ref[...], preferred_element_type=F32)
-        for slot in range(SLOTS):
-            expert = column(2 + slot)
-            logit = jnp.zeros((count, 1), F32)
-            for index in range(EXPERTS):
-                logit = logit + jnp.where(expert == index, logits[:, index : index + 1], 0.0)
-            gate = 1.0 / (1.0 + jnp.exp(-logit))
-            gates_ref[slot] = jnp.broadcast_to(gate * column(1).astype(F32), (count, HD))
+            normed = (x_float * scale * gain_ref[...]).astype(BF16)
+            normed_ref[row : row + block, :] = normed
+            normed = normed.astype(F32)
+            logits = [
+                jnp.sum(normed * router_ref[index : index + 1, :], axis=1, keepdims=True)
+                for index in range(EXPERTS)
+            ]
+            for slot in range(SLOTS):
+                expert = cols_ref[row : row + block, 2 + slot : 3 + slot]
+                logit = jnp.zeros((block, 1), F32)
+                for index in range(EXPERTS):
+                    logit = logit + jnp.where(expert == index, logits[index], 0.0)
+                gate = cols_ref[row : row + block, 1:2].astype(F32) / (1.0 + jnp.exp(-logit))
+                gates_ref[slot, row : row + block, :] = jnp.broadcast_to(gate, (block, HD))
 
     def mask():
         query_index = lax.broadcasted_iota(jnp.int32, (count, count), 0)
         key_index = lax.broadcasted_iota(jnp.int32, (count, count), 1)
-        same = (column(0) == rows_ref[0:1, :]) & (key_index <= query_index)
-        allowed = same & ((rows_ref[1:2, :] == 1) | (key_index == query_index))
+        same = (column(0) == seg_ref[...]) & (key_index <= query_index)
+        allowed = same & ((pad_ref[...] == 1) | (key_index == query_index))
         bias_ref[...] = jnp.where(allowed, 0.0, -1e30)
 
     def weights_of(first, size):
@@ -264,46 +277,42 @@
         )
 
     norm()
-    keep.wait()
-    swap.wait()
+    for copy in keeps + swaps:
+        copy.wait()
     first_round(0)
     mask()
-    first_round(1)
-    route()
-    for step in (2, 3):
+    for step in range(1, HALF):
         first_round(step)
-    first_end()
+    arrived(("whole", "begin", "rest"))
     for step in range(HALF):
         for chunk in (0, 1):
-            turn(0, step, chunk)
-    turn(1, 0, 0)
-    turn(1, 0, 1)
-    arrived(0)
+            first_turn(step, chunk)
+    for chunk in range(4):
+        last_turn(0, chunk)
+    arrived((0,))
     project_keys()
     page_send(0)
-    for step in range(1, HALF):
-        for chunk in (0, 1):
-            turn(1, step, chunk)
+    project_queries(0)
+    last_turn(1, 0)
+    last_turn(1, 1)
+    project_queries(1)
+    last_turn(1, 2)
+    last_turn(1, 3)
     page_take(0)
     page_send(1)
-    turn(2, 0, 0)
-    turn(2, 0, 1)
-    arrived(1)
-    project_queries(0)
-    turn(2, 1, 0)
-    project_queries(1)
-    turn(2, 1, 1)
+    attend(0)
+    last_turn(2, 0)
+    last_turn(2, 1)
+    attend(1)
+    last_turn(2, 2)
+    last_turn(2, 3)
     page_take(1)
     page_send(2)
-    turn(2, 2, 0)
-    attend(0)
-    turn(2, 2, 1)
-    attend(1)
-    turn(2, 3, 0)
-    turn(2, 3, 1)
+    for chunk in range(4):
+        last_turn(3, chunk)
+    arrived((1,))
     page_take(2)
     page_send(3)
-    arrived(2)
 
     def pair_send(index, owner):
         pair_out_ref[index] = project_out(owner).astype(BF16)
@@ -347,14 +356,12 @@
     sine = jnp.concatenate([-sine, sine], axis=1)
     shifts = jnp.repeat(page_shift, count // page_shift.shape[0])
     cols = jnp.stack([seg_row, padding, attn_experts[:, 0], attn_experts[:, 1], shifts], axis=1)
-    rows = jnp.stack([seg_row, padding], axis=0)
-    router = jnp.pad(w_router, ((0, 0), (0, HD - EXPERTS))).astype(BF16)
-    shard = jnp.concatenate([w_kv, w_query, w_out.T], axis=1)
     kv_size, query_size, out_size = w_kv.shape[1], w_query.shape[1], w_out.shape[0]
     parts = ((0, kv_size), (kv_size, query_size), (kv_size + query_size, out_size))
     heads = kv_size // (2 * HD)
     slab = width // (PAIR * CORES)
-    sends = (4 * HALF - 2) + 3 * (8 * HALF - 4)
+    sends = 3 * (2 * HALF - 1) + 2 * (8 * HALF - 4)
+    depth = w_kv.shape[0]
     vmem = pl.BlockSpec(memory_space=pltpu.VMEM)
     attended, cache = pl.pallas_call(
         functools.partial(layer_kernel, parts, heads),
@@ -362,10 +369,10 @@
             jax.ShapeDtypeStruct((count, slab), BF16),
             jax.ShapeDtypeStruct((count, kv_size), BF16),
         ),
-        in_specs=[vmem] * 7 + [pl.BlockSpec(memory_space=pl.ANY)],
+        in_specs=[vmem] * 8 + [pl.BlockSpec(memory_space=pl.ANY)] * 3,
         out_specs=(vmem, vmem),
         scratch_shapes=[
-            pltpu.VMEM((RING, PAIR, RING) + shard.shape, BF16),
+            pltpu.VMEM((RING, PAIR, RING, depth, kv_size + query_size + out_size), BF16),
             pltpu.VMEM((count, width), BF16),
             pltpu.VMEM((count, count), F32),
             pltpu.VMEM((SLOTS, count, HD), F32),
@@ -377,8 +384,8 @@
             pltpu.VMEM((2, count, slab), BF16),
             pltpu.VMEM((count, slab), BF16),
             pltpu.VMEM((count, slab), BF16),
-            pltpu.SemaphoreType.DMA,
-            pltpu.SemaphoreType.DMA((2,)),
+            pltpu.SemaphoreType.DMA((3,)),
+            pltpu.SemaphoreType.DMA((2, 3)),
             pltpu.SemaphoreType.DMA((sends,)),
             pltpu.SemaphoreType.DMA((sends,)),
             pltpu.SemaphoreType.DMA((2, BITS)),
@@ -386,7 +393,19 @@
         ],
         compiler_params=pltpu.CompilerParams(collective_id=0, has_side_effects=True),
         name="layer",
-    )(tokens, gain[None, :], router, cols, rows, cosine, sine, shard)
+    )(
+        tokens,
+        gain[None, :],
+        w_router.T,
+        cols,
+        segment_ids,
+        padding[None, :],
+        cosine,
+        sine,
+        w_kv,
+        w_query,
+        w_out.T,
+    )
     pages = page_shift.shape[0]
     return attended, cache.reshape(pages, count // pages, kv_size)
 

time: 142 us -> 146 us (1.028)
  the two profiles are of different devices: /device:TPU:1 before, /device:TPU:5 now
where the time goes in v3:
time: 146 us
  Pallas kernels  138 us (95%)
  local copies, waits for them, and re-layouts  5.29 us (4%)
  other arithmetic  1.57 us (1%)
    pallas_call x1, Pallas kernels, on_device(): pl.pallas_call(functools.partial(layer_kernel, parts, heads), out_shape=(...  138 us
    unnamed x12, local copies, waits for them, and re-layouts  4.34 us

profile of v3, /device:TPU:5, one launch (start us, length us, event | category | flops | bytes accessed | tf_op | source)
XLA Modules:
  0.0 145.9 jit_solution(13944059626616621282)
XLA Ops:
  0.6 0.0 copy-start.1
  0.7 0.7 copy-done.1
  1.3 0.2 convert_reduce_fusion
  1.5 0.0 copy-start.4
  1.5 0.6 copy-done.4
  2.2 0.1 broadcast_in_dim.12
  2.2 0.0 copy-start.2
  2.2 0.0 copy-start.3
  2.2 0.1 stack_reshape.3
  2.3 0.6 copy-done.2
  2.9 0.0 copy-done.3
  2.9 0.8 copy.18.cols_ref
  3.7 0.5 fusion
  4.3 0.8 pad_maximum_fusion
  5.1 138.4 %layer.1 = (bf16[256,512]{1,0:T(8,128)(2,1)}, bf16[256,512]{1,0:T(8,128)(2,1)}) custom-call(bf16[256,2048]{1,0:T(8,128)(2,1)} %tokens_ref.1, f32[1,2048]{1,0:T(1,128)} %bitcast.13, f32[4,2048]{1,0:T(4,128)} %bitcast.9, s32[256,5]{1,0:T(8,128)} %copy.18.cols_ref, s32[1,256]{1,0:T(1,128)} %seg_ref.1, s32[1,256]{1,0:T(1,128)} %bitcast.14, ...), custom_call_target="tpu_custom_call" | custom-call | tf_op jit(solution)/shard_map/layer/pallas_call | solution.py:366
  143.5 0.0 copy-start
  143.5 1.7 %copy.21 = bf16[256,512]{1,0:T(8,128)(2,1)} copy(bf16[256,512]{1,0:T(8,128)(2,1)} %get-tuple-element.13) | data formatting | bytes 524288
  145.2 0.0 copy-done
  145.2 0.7 copy.22
  (3 shorter events, 0.0 us)
Async XLA Ops:
  0.6 0.7 copy-start.1
  1.5 0.7 copy-start.4
  2.2 0.7 copy-start.2
  2.2 0.7 copy-start.3
  143.5 1.7 %copy-start = (bf16[256,512]{1,0:T(8,128)(2,1)S(1)}, bf16[256,512]{1,0:T(8,128)(2,1)}, u32[]{:S(2)}) copy-start(bf16[256,512]{1,0:T(8,128)(2,1)} %get-tuple-element.5) | copy-start | bytes 786436

commit v4 on v3

--- a/solution.py
+++ b/solution.py
@@ -96,8 +96,6 @@
         copy.start()
         return copy
 
-    (kv_first, kv_size), (query_first, query_size), (out_first, out_size) = parts
-    begin, rest = pl.ds(0, out_first), pl.ds(out_first, out_size)
     keeps, swaps = [], []
     for index, (ref, (first, size)) in enumerate(zip((kv_ref, wide_ref, out_ref), parts)):
         here = full_ref.at[z, x, y, :, pl.ds(first, size)]
@@ -105,55 +103,55 @@
         keep = pltpu.make_async_copy(ref, here, keep_sems.at[index])
         keep.start()
         keeps.append(keep)
+    groups = ((0, parts[2][0]), parts[2])
     issued = []
-    flying = {}
-
-    def send(lane, block):
-        axis, way = lane[0], lane[1]
+
+    def send(axis, way, block):
         slot = len(issued)
         copy = remote(block, block, send_sems.at[slot], recv_sems.at[slot], around[axis, way])
         issued.append(copy)
-        flying[lane] = copy
-
-    def forward(step, hops, lane, block):
-        if step < hops:
-            if step > 0:
-                flying[lane].wait_recv()
-            send(lane, block)
+        return copy
+
+    def single(axis, way, step):
+        back = (-way) * step + RING
+        if axis == "z":
+            return full_ref.at[(z + back) % RING, 0, y]
+        return full_ref.at[z, 1, (y + back) % RING]
+
+    def several(axis, way, step, part, chunk):
+        back = (-way) * step + RING
+        columns = pl.ds(*groups[part])
+        run = pl.ds(HALF * chunk, HALF)
+        if axis == "y":
+            return full_ref.at[run, 0, (y + back) % RING, :, columns]
+        return full_ref.at[(z + back) % RING, 1, run, :, columns]
+
+    flying = {}
+    streams = [(axis, way) for way in (1, -1) for axis in ("z", "y")]
 
     def first_round(step):
-        for way in (1, -1):
-            back = (-way) * step + RING
-            hops = HALF if way == 1 else HALF - 1
-            there = (y + back) % RING
-            forward(step, hops, ("y", way, "whole"), full_ref.at[z, 1, there])
-            forward(step, hops, ("z", way, "begin"), full_ref.at[(z + back) % RING, 0, y, :, begin])
-            forward(step, hops, ("y", way, "rest"), full_ref.at[z, 0, there, :, rest])
-
-    def first_turn(step, chunk):
-        run = pl.ds(HALF * chunk, HALF)
-        for way in (1, -1):
-            back = (-way) * step + RING
-            hops = HALF if (way == 1) == (chunk == 0) else HALF - 1
-            forward(step, hops, ("z", way, 0, chunk), full_ref.at[(z + back) % RING, 1, run, :, begin])
-            forward(step, hops, ("y", way, 0, chunk), full_ref.at[run, 0, (y + back) % RING, :, begin])
-
-    def last_turn(step, chunk):
-        run = pl.ds(HALF * (chunk // 2), HALF)
-        for way in (1, -1):
-            back = (-way) * step + RING
-            hops = HALF if (way == 1) == (chunk % 2 == 0) else HALF - 1
-            forward(
-                step,
-                hops,
-                ("z", way, 1, chunk),
-                full_ref.at[(z + back) % RING, chunk % 2, run, :, rest],
-            )
-
-    def arrived(kind):
-        for lane, copy in flying.items():
-            if lane[2] in kind:
-                copy.wait_recv()
+        for axis, way in streams:
+            if step < (HALF if way == 1 else HALF - 1):
+                if step > 0:
+                    flying[axis, way].wait_recv()
+                flying[axis, way] = send(axis, way, single(axis, way, step))
+
+    def first_end():
+        for stream in streams:
+            flying[stream].wait_recv()
+
+    def turn(part, step, chunk):
+        for axis, way in streams:
+            if step < (HALF if (way == 1) == (chunk == 0) else HALF - 1):
+                lane = (axis, way, part, chunk)
+                if step > 0:
+                    flying[lane].wait_recv()
+                flying[lane] = send(axis, way, several(axis, way, step, part, chunk))
+
+    def arrived(part):
+        for chunk in (0, 1):
+            for axis, way in streams:
+                flying[axis, way, part, chunk].wait_recv()
 
     def column(index):
         return cols_ref[:, index : index + 1]
@@ -281,38 +279,33 @@
         copy.wait()
     first_round(0)
     mask()
-    for step in range(1, HALF):
+    first_round(1)
+    for step in (2, 3):
         first_round(step)
-    arrived(("whole", "begin", "rest"))
+    first_end()
     for step in range(HALF):
         for chunk in (0, 1):
-            first_turn(step, chunk)
-    for chunk in range(4):
-        last_turn(0, chunk)
-    arrived((0,))
+            turn(0, step, chunk)
+    turn(1, 0, 0)
+    turn(1, 0, 1)
+    arrived(0)
     project_keys()
     page_send(0)
     project_queries(0)
-    last_turn(1, 0)
-    last_turn(1, 1)
+    turn(1, 1, 0)
+    turn(1, 1, 1)
     project_queries(1)
-    last_turn(1, 2)
-    last_turn(1, 3)
     page_take(0)
     page_send(1)
     attend(0)
-    last_turn(2, 0)
-    last_turn(2, 1)
+    turn(1, 2, 0)
+    turn(1, 2, 1)
     attend(1)
-    last_turn(2, 2)
-    last_turn(2, 3)
+    turn(1, 3, 0)
+    turn(1, 3, 1)
     page_take(1)
     page_send(2)
-    for chunk in range(4):
-        last_turn(3, chunk)
-    arrived((1,))
-    page_take(2)
-    page_send(3)
+    arrived(1)
 
     def pair_send(index, owner):
         pair_out_ref[index] = project_out(owner).astype(BF16)
@@ -333,10 +326,12 @@
     near = project_out(low * CORES + core)
     pairs[1].wait_recv()
     near = near + pair_in_ref[1].astype(F32)
-    page_take(3)
+    page_take(2)
+    page_send(3)
     far_copy.wait_recv()
     attended_ref[...] = (near + far_in_ref[...].astype(F32)).astype(BF16)
 
+    page_take(3)
     for copy in issued + moves + pairs + [far_copy]:
         copy.wait_send()
 
@@ -359,9 +354,9 @@
     kv_size, query_size, out_size = w_kv.shape[1], w_query.shape[1], w_out.shape[0]
     parts = ((0, kv_size), (kv_size, query_size), (kv_size + query_size, out_size))
     heads = kv_size // (2 * HD)
+    depth = w_kv.shape[0]
     slab = width // (PAIR * CORES)
-    sends = 3 * (2 * HALF - 1) + 2 * (8 * HALF - 4)
-    depth = w_kv.shape[0]
+    sends = (4 * HALF - 2) + 2 * (8 * HALF - 4)
     vmem = pl.BlockSpec(memory_space=pltpu.VMEM)
     attended, cache = pl.pallas_call(
         functools.partial(layer_kernel, parts, heads),

time: 146 us -> 132 us (0.904)
  the two profiles are of different devices: /device:TPU:5 before, /device:TPU:1 now
where the time goes in v4:
time: 132 us; the launch traced here: 131 us
  Pallas kernels  124 us (94%)
  local copies, waits for them, and re-layouts  5.29 us (4%)
  other arithmetic  1.57 us (1%)
    pallas_call x1, Pallas kernels, on_device(): pl.pallas_call(functools.partial(layer_kernel, parts, heads), out_shape=(...  124 us
    unnamed x12, local copies, waits for them, and re-layouts  4.34 us

profile of v4, /device:TPU:1, one launch (start us, length us, event | category | flops | bytes accessed | tf_op | source)
XLA Modules:
  0.0 131.5 jit_solution(8314332286303256826)
XLA Ops:
  0.6 0.0 copy-start.1
  0.7 0.7 copy-done.1
  1.3 0.2 convert_reduce_fusion
  1.5 0.0 copy-start.4
  1.5 0.6 copy-done.4
  2.2 0.1 broadcast_in_dim.12
  2.2 0.0 copy-start.2
  2.2 0.0 copy-start.3
  2.2 0.1 stack_reshape.3
  2.3 0.6 copy-done.2
  2.9 0.0 copy-done.3
  2.9 0.8 copy.18.cols_ref
  3.7 0.5 fusion
  4.3 0.8 pad_maximum_fusion
  5.1 123.9 %layer.1 = (bf16[256,512]{1,0:T(8,128)(2,1)}, bf16[256,512]{1,0:T(8,128)(2,1)}) custom-call(bf16[256,2048]{1,0:T(8,128)(2,1)} %tokens_ref.1, f32[1,2048]{1,0:T(1,128)} %bitcast.13, f32[4,2048]{1,0:T(4,128)} %bitcast.9, s32[256,5]{1,0:T(8,128)} %copy.18.cols_ref, s32[1,256]{1,0:T(1,128)} %seg_ref.1, s32[1,256]{1,0:T(1,128)} %bitcast.14, ...), custom_call_target="tpu_custom_call" | custom-call | tf_op jit(solution)/shard_map/layer/pallas_call | solution.py:361
  129.1 0.0 copy-start
  129.1 1.7 %copy.21 = bf16[256,512]{1,0:T(8,128)(2,1)} copy(bf16[256,512]{1,0:T(8,128)(2,1)} %get-tuple-element.13) | data formatting | bytes 524288
  130.8 0.0 copy-done
  130.8 0.7 copy.22
  (3 shorter events, 0.0 us)
Async XLA Ops:
  0.6 0.7 copy-start.1
  1.5 0.7 copy-start.4
  2.2 0.7 copy-start.2
  2.2 0.7 copy-start.3
  129.1 1.7 %copy-start = (bf16[256,512]{1,0:T(8,128)(2,1)S(1)}, bf16[256,512]{1,0:T(8,128)(2,1)}, u32[]{:S(2)}) copy-start(bf16[256,512]{1,0:T(8,128)(2,1)} %get-tuple-element.5) | copy-start | bytes 786436

commit v5 on v4

--- a/solution.py
+++ b/solution.py
@@ -74,7 +74,7 @@
         ("y", 1): place(z, x, y + 1),
         ("y", -1): place(z, x, y - 1),
     }
-    levels = [2**level for level in reversed(range(BITS))]
+    levels = [2, 4, 8, 1]
     ahead = [{"req": (me + shift) % REQ} for shift in levels]
     behind = [{"req": (me + REQ - shift) % REQ} for shift in levels]
 

time: 132 us -> 135 us (1.023)
  Pallas kernels: 124 us -> 127 us
    pallas_call x1, Pallas kernels: 124 us -> 127 us  [on_device(): pl.pallas_call(functools.partial(layer_kernel, parts, heads), out_shape=(...]
where the time goes in v5:
time: 135 us
  Pallas kernels  127 us (94%)
  local copies, waits for them, and re-layouts  5.29 us (4%)
  other arithmetic  1.57 us (1%)
    pallas_call x1, Pallas kernels, on_device(): pl.pallas_call(functools.partial(layer_kernel, parts, heads), out_shape=(...  127 us
    unnamed x12, local copies, waits for them, and re-layouts  4.34 us

profile of v5, /device:TPU:1, one launch (start us, length us, event | category | flops | bytes accessed | tf_op | source)
XLA Modules:
  0.0 134.8 jit_solution(10661472923445514116)
XLA Ops:
  0.6 0.0 copy-start.1
  0.7 0.7 copy-done.1
  1.3 0.2 convert_reduce_fusion
  1.5 0.0 copy-start.4
  1.5 0.6 copy-done.4
  2.2 0.1 broadcast_in_dim.12
  2.2 0.0 copy-start.2
  2.2 0.0 copy-start.3
  2.2 0.1 stack_reshape.3
  2.3 0.6 copy-done.2
  2.9 0.0 copy-done.3
  2.9 0.8 copy.18.cols_ref
  3.7 0.5 fusion
  4.3 0.8 pad_maximum_fusion
  5.1 127.3 %layer.1 = (bf16[256,512]{1,0:T(8,128)(2,1)}, bf16[256,512]{1,0:T(8,128)(2,1)}) custom-call(bf16[256,2048]{1,0:T(8,128)(2,1)} %tokens_ref.1, f32[1,2048]{1,0:T(1,128)} %bitcast.13, f32[4,2048]{1,0:T(4,128)} %bitcast.9, s32[256,5]{1,0:T(8,128)} %copy.18.cols_ref, s32[1,256]{1,0:T(1,128)} %seg_ref.1, s32[1,256]{1,0:T(1,128)} %bitcast.14, ...), custom_call_target="tpu_custom_call" | custom-call | tf_op jit(solution)/shard_map/layer/pallas_call | solution.py:361
  132.4 0.0 copy-start
  132.4 1.7 %copy.21 = bf16[256,512]{1,0:T(8,128)(2,1)} copy(bf16[256,512]{1,0:T(8,128)(2,1)} %get-tuple-element.13) | data formatting | bytes 524288
  134.1 0.0 copy-done
  134.1 0.7 copy.22
  (3 shorter events, 0.0 us)
Async XLA Ops:
  0.6 0.7 copy-start.1
  1.5 0.7 copy-start.4
  2.2 0.7 copy-start.2
  2.2 0.7 copy-start.3
  132.4 1.7 %copy-start = (bf16[256,512]{1,0:T(8,128)(2,1)S(1)}, bf16[256,512]{1,0:T(8,128)(2,1)}, u32[]{:S(2)}) copy-start(bf16[256,512]{1,0:T(8,128)(2,1)} %get-tuple-element.5) | copy-start | bytes 786436
